TPU v7x, 1024 devices: a whole 4x8x16 slice. The times are simulated.
1024 devices in a mesh: seq: 16 (over y, x_hi), section: 16 (over z), mp: 4 (over x_lo, core).
Axes of the slice: x: 4 (x_hi: 2, x_lo: 2; x = x_hi * 2 + x_lo), y: 8, z: 16, core: 2. Of those that a mesh axis runs over, the one named last changes fastest.
Arguments:
- enc_rows: bfloat16 [16, 4096, 512], P('section', 'seq'), may hold values from -6 to 6
- proj_weight: bfloat16 [512, 8192], P(None, 'mp'), may hold values from -0.25 to 0.25
- row_owner: int32 [16, 4096], P('section', 'seq'), may hold values from -1 to 15, as said below
- grad_in: bfloat16 [16, 4096, 8192], P('section', 'seq', 'mp'), may hold values from -3 to 3
- adapter_gain: float32 [16, 8192], P('section', 'mp'), may hold values from 0.25 to 1.75
- adapter_down: bfloat16 [16, 64, 8192], P('section', None, 'mp'), may hold values from -0.375 to 0.375
- adapter_up: bfloat16 [16, 64, 8192], P('section', None, 'mp'), may hold values from -0.0625 to 0.0625
Outputs:
- soft_tokens: bfloat16 [16, 4096, 8192], P('section', 'seq', 'mp')
- enc_grad: float32 [16, 4096, 512], P('section', 'seq', 'mp')
Inputs may be any that keep to these rules, and one draw needn't show every extreme that they name: row_owner[s, r] is the reader device along seq of encoder row r of micro-batch s, or -1 for an empty row. Every reader receives 16 to 256 rows of a micro-batch, and one reader exactly 256. One encoder device holds at most 16 rows for one reader, and exactly 16 for that fullest reader.
All inputs are finite; a program needn't handle non-finite values.
Results may differ from a plain program's by a relative error of at most 0.0061.
Values may be sent and summed in bfloat16 or wider, within the bound.
No kernel may reach another device: no remote copies, remote signals or barrier semaphores. Data moves between devices by JAX's collectives and lax.ppermute only.
A program may use at most 32 MiB of HBM per device.

v0:
```python
import jax
import jax.numpy as jnp
from jax import lax
from jax.sharding import PartitionSpec as P

TICKS = 2


def from_behind(value, axis, steps):
    count = lax.axis_size(axis)
    pairs = [(source, (source + steps) % count) for source in range(count)]
    return lax.ppermute(value, axis, pairs)


def pick_rows(values, row_index, keep_mask):
    picked = jnp.take(values, jnp.minimum(row_index, values.shape[0] - 1), axis=0)
    return jnp.where(keep_mask[:, None], picked, jnp.zeros_like(picked))


def adapter_back(carried, gain_row, down_rows, up_rows):
    partial_low = lax.dot_general(
        up_rows, carried, (((1,), (1,)), ((), ())), preferred_element_type=jnp.float32
    )
    reduced = lax.psum(partial_low, "mp").astype(jnp.bfloat16)
    spread = lax.dot_general(
        reduced, down_rows, (((0,), (0,)), ((), ())), preferred_element_type=jnp.float32
    )
    return (carried.astype(jnp.float32) + gain_row[None, :] * spread).astype(jnp.bfloat16)


def on_device(enc_rows, proj_weight, row_owner, grad_in, adapter_gain, adapter_down, adapter_up):
    readers = lax.axis_size("seq")
    owners = row_owner[0]
    slot_count = owners.shape[0]
    per_peer = slot_count // readers
    matches = (owners[:, None] == jnp.arange(readers, dtype=jnp.int32)[None, :]).astype(jnp.int32)
    before = jnp.cumsum(matches, axis=0) - matches
    order_rank = jnp.sum(matches * before, axis=1)
    live_in = owners >= 0
    target = jnp.where(live_in, owners * per_peer + order_rank, slot_count)
    source = (
        jnp.full((slot_count + 1,), slot_count, jnp.int32)
        .at[target]
        .set(jnp.arange(slot_count, dtype=jnp.int32))[:slot_count]
    )
    live_out = source < slot_count
    enc_block = enc_rows[0]
    projected = jnp.dot(enc_block, proj_weight, preferred_element_type=jnp.float32).astype(
        jnp.bfloat16
    )
    outgoing = pick_rows(projected, source, live_out)
    soft_block = lax.all_to_all(outgoing, "seq", split_axis=0, concat_axis=0, tiled=True)
    gain_row = adapter_gain[0]
    down_rows = adapter_down[0]
    up_rows = adapter_up[0]
    carried = grad_in[0]
    for tick_index in range(TICKS + 1):
        carried = adapter_back(carried, gain_row, down_rows, up_rows)
        if tick_index < TICKS:
            carried = from_behind(carried, "section", -1)
    returned = lax.all_to_all(carried, "seq", split_axis=0, concat_axis=0, tiled=True)
    own_grads = pick_rows(returned, target, live_in)
    partial_rows = lax.dot_general(
        own_grads, proj_weight, (((1,), (1,)), ((), ())), preferred_element_type=jnp.float32
    )
    row_grads = lax.psum_scatter(partial_rows, "mp", scatter_dimension=1, tiled=True)
    return (soft_block[None], row_grads[None])


def solution(mesh):
    placed = (
        P("section", "seq", None),
        P(None, "mp"),
        P("section", "seq"),
        P("section", "seq", "mp"),
        P("section", "mp"),
        P("section", None, "mp"),
        P("section", None, "mp"),
    )
    return jax.shard_map(
        on_device,
        mesh=mesh,
        in_specs=placed,
        out_specs=(P("section", "seq", "mp"), P("section", "seq", "mp")),
        check_vma=False,
    )
```

profile of v0, /device:TPU:1, one launch (start us, length us, event | category | flops | bytes accessed | tf_op | source)
XLA Modules:
  0.0 205.8 jit_solution(8025791955081929983)
XLA Ops:
  7.2 0.0 copy-start
  7.2 1.9 fusion.2
  9.1 0.0 copy-start.1
  9.1 0.0 copy-start.5
  9.1 24.1 %psum.21 = bf16[64,256]{1,0:T(8,128)(2,1)S(1)} all-reduce(f32[64,256]{1,0:T(8,128)S(1)} %fusion.2), channel_id=1, replica_groups=mesh['seq'=16,'section'=16,'mp'=4] {'mp'}, use_global_device_ids=true, to_apply=%region_4.6 | all-reduce | flops 16384 | bytes 98304 | tf_op jit(solution)/shard_map/psum | solution.py:24
  33.2 0.0 copy-start.2
  33.2 1.8 fusion.1
  35.0 5.7 %collective-permute-start = (bf16[256,2048]{1,0:T(8,128)(2,1)S(1)}, bf16[256,2048]{1,0:T(8,128)(2,1)S(1)}, u32[]{:S(2)}, u32[]{:S(2)}) collective-permute-start(bf16[256,2048]{1,0:T(8,128)(2,1)S(1)} %fusion.1), channel_id=1, source_target_pairs={{0,60},{4,0},{8,4},{12,8},{16,12},{20,16},{24,20},{28,24},{32,28},... | collective-permute-start | bytes 3145736 | tf_op jit(solution)/shard_map/ppermute | solution.py:12
  40.7 20.7 %collective-permute-done = bf16[256,2048]{1,0:T(8,128)(2,1)S(1)} collective-permute-done((bf16[256,2048]{1,0:T(8,128)(2,1)S(1)}, bf16[256,2048]{1,0:T(8,128)(2,1)S(1)}, u32[]{:S(2)}, u32[]{:S(2)}) %collective-permute-start) | collective-permute-done | bytes 1048608 | tf_op jit(solution)/shard_map/ppermute | solution.py:12
  61.5 0.0 copy-done.2
  61.5 0.4 convolution_bitcast_fusion.1
  61.9 14.8 %psum.22 = bf16[64,256]{0,1:T(8,128)(2,1)} all-reduce(f32[64,256]{0,1:T(8,128)S(1)} %convolution_bitcast_fusion.1), channel_id=1, replica_groups=mesh['seq'=16,'section'=16,'mp'=4] {'mp'}, use_global_device_ids=true, to_apply=%region_5.7 | all-reduce | flops 16384 | bytes 98304 | tf_op jit(solution)/shard_map/psum | solution.py:24
  76.7 0.0 copy-done.1
  76.7 0.0 copy-done.5
  76.7 0.0 copy-start.3
  76.7 1.3 add_convert_fusion.1
  78.0 5.3 %collective-permute-start.1 = (bf16[256,2048]{1,0:T(8,128)(2,1)S(1)}, bf16[256,2048]{1,0:T(8,128)(2,1)S(1)}, u32[]{:S(2)}, u32[]{:S(2)}) collective-permute-start(bf16[256,2048]{1,0:T(8,128)(2,1)S(1)} %add_convert_fusion.1), channel_id=1, source_target_pairs={{0,60},{4,0},{8,4},{12,8},{16,12},{20,16},{24,20},{28,24},{32,28},... | collective-permute-start | bytes 3145736 | tf_op jit(solution)/shard_map/ppermute | solution.py:12
  83.4 22.0 %collective-permute-done.1 = bf16[256,2048]{1,0:T(8,128)(2,1)S(1)} collective-permute-done((bf16[256,2048]{1,0:T(8,128)(2,1)S(1)}, bf16[256,2048]{1,0:T(8,128)(2,1)S(1)}, u32[]{:S(2)}, u32[]{:S(2)}) %collective-permute-start.1) | collective-permute-done | bytes 1048608 | tf_op jit(solution)/shard_map/ppermute | solution.py:12
  105.4 0.0 copy-done.3
  105.4 0.4 convolution_bitcast_fusion
  105.8 12.4 %psum.23 = bf16[64,256]{0,1:T(8,128)(2,1)} all-reduce(f32[64,256]{0,1:T(8,128)S(1)} %convolution_bitcast_fusion), channel_id=1, replica_groups=mesh['seq'=16,'section'=16,'mp'=4] {'mp'}, use_global_device_ids=true, to_apply=%region_6.8 | all-reduce | flops 16384 | bytes 98304 | tf_op jit(solution)/shard_map/psum | solution.py:24
  118.2 0.0 copy-start.6
  118.2 2.3 %add_convert_fusion = bf16[256,2048]{1,0:T(8,128)(2,1)} fusion(bf16[256,2048]{1,0:T(8,128)(2,1)S(1)} %collective-permute-done.1, f32[2048]{0:T(1024)S(1)} %bitcast.74, bf16[1,64,2048]{2,1,0:T(8,128)(2,1)S(1)} %copy-done.1, bf16[64,256]{0,1:T(8,128)(2,1)} %psum.23), kind=kOutput, calls=%fused_computation.9 | convolution fusion | flops 69206016 | bytes 2400256 | tf_op jit(solution)/shard_map/dot_general | solution.py:25
  120.5 0.0 copy-start.4
  120.5 9.0 %all-to-all-start.1 = ((bf16[16,16,2048]{2,1,0:T(8,128)(2,1)}), bf16[16,16,2048]{2,1,0:T(8,128)(2,1)S(1)}, u32[]{:S(2)}, u32[]{:S(2)}) async-start(bf16[16,16,2048]{2,1,0:T(8,128)(2,1)} %bitcast.70), calls=%async_computation.1 | async-start | bytes 2097152 | tf_op jit(solution)/shard_map/all_to_all | solution.py:61
  129.5 0.0 copy-done.6
  129.6 0.6 reduce-window.6
  130.2 0.2 slice_reduce_fusion
  130.4 0.1 fusion.21
  130.5 1.4 scatter_custom_fusion
  131.9 0.0 copy-done
  131.9 0.0 copy-done.4
  132.0 1.7 convolution_convert_fusion
  133.6 4.8 %gather_fusion = bf16[256,2048]{1,0:T(8,128)(2,1)} fusion(bf16[256,2048]{1,0:T(8,128)(2,1)} %convolution_convert_fusion, s32[1024]{0:T(1024)S(1)} %pad_clamp_fusion.1), kind=kCustom, calls=%fused_computation.clone | custom fusion | bytes 2098176 | tf_op jit(solution)/shard_map/jit(_take)/gather | solution.py:16
  138.4 2.4 %select_select_fusion.2 = bf16[256,2048]{1,0:T(8,128)(2,1)} fusion(bf16[256,2048]{1,0:T(8,128)(2,1)} %gather_fusion, pred[256]{0:T(512)(128)(4,1)S(1)} %get-tuple-element.5, pred[256]{0:T(512)(128)(4,1)S(1)} %get-tuple-element.7), kind=kLoop, calls=%fused_computation.17 | loop fusion | flops 1048576 | bytes 2097664 | tf_op jit(solution)/shard_map/jit(_where)/select_n | solution.py:17
  140.8 14.7 %all-to-all-done.1 = bf16[16,16,2048]{2,1,0:T(8,128)(2,1)S(1)} async-done(((bf16[16,16,2048]{2,1,0:T(8,128)(2,1)}), bf16[16,16,2048]{2,1,0:T(8,128)(2,1)S(1)}, u32[]{:S(2)}, u32[]{:S(2)}) %all-to-all-start.1) | async-done | bytes 1048608 | tf_op jit(solution)/shard_map/all_to_all | solution.py:61
  155.5 7.2 %all-to-all-start = ((bf16[16,16,2048]{2,1,0:T(8,128)(2,1)}), bf16[16,16,2048]{2,1,0:T(8,128)(2,1)}, u32[]{:S(2)}, u32[]{:S(2)}) async-start(bf16[16,16,2048]{2,1,0:T(8,128)(2,1)} %bitcast.71), calls=%async_computation | async-start | bytes 2097152 | tf_op jit(solution)/shard_map/all_to_all | solution.py:52
  162.8 0.0 reduce-scatter.2.cloned.1.call-start
  162.8 2.4 %gather_fusion.1 = bf16[256,2048]{1,0:T(8,128)(2,1)} fusion(bf16[256,2048]{1,0:T(8,128)(2,1)S(1)} %bitcast.69, s32[1024]{0:T(1024)S(1)} %pad_clamp_fusion), kind=kCustom, calls=%fused_computation.1.clone | custom fusion | bytes 2098176 | tf_op jit(solution)/shard_map/jit(_take)/gather | solution.py:16
  165.2 2.8 %fusion.4 = f32[256,512]{1,0:T(8,128)} fusion(bf16[512,2048]{1,0:T(8,128)(2,1)S(1)} %copy-done, bf16[256,2048]{1,0:T(8,128)(2,1)} %gather_fusion.1, pred[256]{0:T(512)(128)(4,1)S(1)} %get-tuple-element.3, pred[256]{0:T(512)(128)(4,1)S(1)} %get-tuple-element.8), kind=kOutput, calls=%fused_computation.16 | convolution fusion | flops 537919488 | bytes 3670528 | tf_op jit(solution)/shard_map/dot_general | solution.py:63
  168.0 0.0 reduce-scatter.2.cloned.1.call-update
  168.0 20.7 %all-to-all-done = bf16[16,16,2048]{2,1,0:T(8,128)(2,1)} async-done(((bf16[16,16,2048]{2,1,0:T(8,128)(2,1)}), bf16[16,16,2048]{2,1,0:T(8,128)(2,1)}, u32[]{:S(2)}, u32[]{:S(2)}) %all-to-all-start) | async-done | bytes 1048608 | tf_op jit(solution)/shard_map/all_to_all | solution.py:52
  188.8 7.9 %reduce-scatter.2.cloned.1.call-done = f32[256,128]{1,0:T(8,128)} async-done(((f32[256,512]{1,0:T(8,128)}), f32[256,128]{1,0:T(8,128)}) %reduce-scatter.2.cloned.1.call-update) | async-done | bytes 131088 | tf_op jit(solution)/shard_map/reduce_scatter | solution.py:66
  196.7 2.3 %copy.13 = bf16[1,256,2048]{2,1,0:T(8,128)(2,1)} copy(bf16[1,256,2048]{2,1,0:T(8,128)(2,1)} %bitcast.9) | data formatting | bytes 2097152
  (9 shorter events, 0.1 us)
Async XLA Ops:
  7.2 124.8 %copy-start = (bf16[512,2048]{1,0:T(8,128)(2,1)S(1)}, bf16[512,2048]{1,0:T(8,128)(2,1)}, u32[]{:S(2)}) copy-start(bf16[512,2048]{1,0:T(8,128)(2,1)} %param.10) | copy-start | bytes 6291460
  9.1 67.7 %copy-start.1 = (bf16[1,64,2048]{2,1,0:T(8,128)(2,1)S(1)}, bf16[1,64,2048]{2,1,0:T(8,128)(2,1)}, u32[]{:S(2)}) copy-start(bf16[1,64,2048]{2,1,0:T(8,128)(2,1)} %param.14) | copy-start | bytes 786436
  9.1 67.7 %copy-start.5 = (f32[1,2048]{1,0:T(1,128)S(1)}, f32[1,2048]{1,0:T(1,128)}, u32[]{:S(2)}) copy-start(f32[1,2048]{1,0:T(1,128)} %param.13) | copy-start | bytes 24580
  33.2 28.3 %copy-start.2 = (bf16[1,64,2048]{2,1,0:T(8,128)(2,1)S(1)}, bf16[1,64,2048]{2,1,0:T(8,128)(2,1)}, u32[]{:S(2)}) copy-start(bf16[1,64,2048]{2,1,0:T(8,128)(2,1)} %param.15) | copy-start | bytes 786436
  35.0 26.5 %collective-permute-start = (bf16[256,2048]{1,0:T(8,128)(2,1)S(1)}, bf16[256,2048]{1,0:T(8,128)(2,1)S(1)}, u32[]{:S(2)}, u32[]{:S(2)}) collective-permute-start(bf16[256,2048]{1,0:T(8,128)(2,1)S(1)} %fusion.1), channel_id=1, source_target_pairs={{0,60},{4,0},{8,4},{12,8},{16,12},{20,16},{24,20},{28,24},{32,28},... | collective-permute-start | bytes 3145736 | tf_op jit(solution)/shard_map/ppermute | solution.py:12
  76.7 28.7 %copy-start.3 = (bf16[1,64,2048]{2,1,0:T(8,128)(2,1)S(1)}, bf16[1,64,2048]{2,1,0:T(8,128)(2,1)}, u32[]{:S(2)}) copy-start(bf16[1,64,2048]{2,1,0:T(8,128)(2,1)} %param.15) | copy-start | bytes 786436
  78.0 27.4 %collective-permute-start.1 = (bf16[256,2048]{1,0:T(8,128)(2,1)S(1)}, bf16[256,2048]{1,0:T(8,128)(2,1)S(1)}, u32[]{:S(2)}, u32[]{:S(2)}) collective-permute-start(bf16[256,2048]{1,0:T(8,128)(2,1)S(1)} %add_convert_fusion.1), channel_id=1, source_target_pairs={{0,60},{4,0},{8,4},{12,8},{16,12},{20,16},{24,20},{28,24},{32,28},... | collective-permute-start | bytes 3145736 | tf_op jit(solution)/shard_map/ppermute | solution.py:12
  118.2 11.3 %copy-start.6 = (s32[1,256]{1,0:T(1,128)S(1)}, s32[1,256]{1,0:T(1,128)}, u32[]{:S(2)}) copy-start(s32[1,256]{1,0:T(1,128)} %param.11) | copy-start | bytes 3076
  120.5 11.5 %copy-start.4 = (bf16[1,256,512]{2,1,0:T(8,128)(2,1)S(1)}, bf16[1,256,512]{2,1,0:T(8,128)(2,1)}, u32[]{:S(2)}) copy-start(bf16[1,256,512]{2,1,0:T(8,128)(2,1)} %param.9) | copy-start | bytes 786436
  120.5 35.0 %all-to-all-start.1 = ((bf16[16,16,2048]{2,1,0:T(8,128)(2,1)}), bf16[16,16,2048]{2,1,0:T(8,128)(2,1)S(1)}, u32[]{:S(2)}, u32[]{:S(2)}) async-start(bf16[16,16,2048]{2,1,0:T(8,128)(2,1)} %bitcast.70), calls=%async_computation.1 | async-start | bytes 2097152 | tf_op jit(solution)/shard_map/all_to_all | solution.py:61
  155.5 33.3 %all-to-all-start = ((bf16[16,16,2048]{2,1,0:T(8,128)(2,1)}), bf16[16,16,2048]{2,1,0:T(8,128)(2,1)}, u32[]{:S(2)}, u32[]{:S(2)}) async-start(bf16[16,16,2048]{2,1,0:T(8,128)(2,1)} %bitcast.71), calls=%async_computation | async-start | bytes 2097152 | tf_op jit(solution)/shard_map/all_to_all | solution.py:52
  162.8 33.9 %reduce-scatter.2.cloned.1.call-start = ((), (), s32[]{:S(2)}) async-start(), calls=%async_computation.3 | async-start | bytes 655360 | tf_op jit(solution)/shard_map/reduce_scatter | solution.py:66
Sparse Core Ops, SparseCore 0:
  168.2 28.4 reduce-scatter.1
where the time goes:
time: 206 us
  waiting for transfers between devices  86.1 us (42%)
  blocking collectives  51.3 us (25%)
  starting transfers between devices  27.4 us (13%)
  between operations  14.2 us (7%)
  matrix products  12.5 us (6%)
  local copies, waits for them, and re-layouts  11.1 us (5%)
  other arithmetic  3.16 us (2%)
    psum x3, blocking collectives, adapter_back(): reduced = lax.psum(partial_low, 'mp').astype(jnp.bfloat16)  51.3 us
    ppermute x2, waiting for transfers between devices, from_behind(): return lax.ppermute(value, axis, pairs)  42.8 us
    all_to_all x1, waiting for transfers between devices, on_device(): lax.all_to_all(outgoing, 'seq', split_axis=0, concat_axis=0, tiled=True)  20.7 us
    all_to_all x1, waiting for transfers between devices, on_device(): lax.all_to_all(carried, 'seq', split_axis=0, concat_axis=0, tiled=True)  14.7 us
    ppermute x2, starting transfers between devices, from_behind(): return lax.ppermute(value, axis, pairs)  11 us
    all_to_all x1, starting transfers between devices, on_device(): lax.all_to_all(carried, 'seq', split_axis=0, concat_axis=0, tiled=True)  9.05 us
    reduce_scatter x1, waiting for transfers between devices, on_device(): lax.psum_scatter(partial_rows, 'mp', scatter_dimension=1, tiled=True)  7.92 us
    all_to_all x1, starting transfers between devices, on_device(): lax.all_to_all(outgoing, 'seq', split_axis=0, concat_axis=0, tiled=True)  7.24 us
  transfers between devices with their start and end apart: 5, of which 5 were waited for; matrix products, arithmetic and copies ran while one was open for 8% of the time, Pallas kernels for 0%

commit v1 on v0

v1 whole, which is shorter than its diff:
```python
import jax
import jax.numpy as jnp
from jax import lax
from jax.sharding import PartitionSpec as P

BF16 = jnp.bfloat16
F32 = jnp.float32


def send_along(value, axis, steps):
    count = lax.axis_size(axis)
    return lax.ppermute(value, axis, [(i, (i + steps) % count) for i in range(count)])


def dot(a, b, contract_a, contract_b):
    return lax.dot_general(a, b, (((contract_a,), (contract_b,)), ((), ())), preferred_element_type=F32)


def slots_of_rows(owners, readers, per_peer):
    rows = owners.shape[1]
    reader = lax.broadcasted_iota(jnp.int32, (readers, rows), 0)
    is_owner = reader == owners
    matches = is_owner.astype(BF16)
    earlier = (
        lax.broadcasted_iota(jnp.int32, (rows, rows), 0) < lax.broadcasted_iota(jnp.int32, (rows, rows), 1)
    ).astype(BF16)
    before = dot(matches, earlier, 1, 0)
    rank = jnp.sum(jnp.where(is_owner, before, 0.0), axis=0, keepdims=True).astype(jnp.int32)
    return jnp.where(owners >= 0, owners * per_peer + rank, -1)


def on_device(enc_rows, proj_weight, row_owner, grad_in, adapter_gain, adapter_down, adapter_up):
    readers = lax.axis_size("seq")
    feature_parts = lax.axis_size("mp")
    enc_block, grad = enc_rows[0], grad_in[0]
    slots = grad.shape[0]
    per_peer = slots // readers
    graph_width = enc_block.shape[1]
    part = graph_width // feature_parts
    up = adapter_up[0]
    rank = up.shape[0]

    up_one = send_along(up, "section", 1)
    up_zero = send_along(up, "section", 2)

    down = (adapter_down[0].astype(F32) * adapter_gain).astype(BF16)
    low_part = dot(up, grad, 1, 1)
    through_part = dot(down, proj_weight, 1, 1).astype(BF16)
    first = jnp.concatenate([low_part.astype(BF16), through_part], axis=1)
    first = jnp.sum(lax.all_gather(first, "mp").astype(F32), axis=0).astype(BF16)
    low_two, through = first[:, :slots], first[:, slots:]
    through_zero = send_along(through, "section", 2)
    carried = (grad.astype(F32) + dot(low_two, down, 0, 0)).astype(BF16)

    low_one_part = dot(up_one, carried, 1, 1).astype(BF16)
    cross_part = dot(down, up_one, 1, 1).astype(BF16)
    from_one = send_along(jnp.concatenate([through_part, cross_part], axis=1), "section", 1)
    low_one = jnp.sum(lax.all_gather(low_one_part, "mp").astype(F32), axis=0).astype(BF16)
    through_one_part, cross_one_part = from_one[:, :graph_width], from_one[:, graph_width:]
    low_zero_part = (dot(carried, up_zero, 1, 1) + dot(low_one, cross_one_part, 0, 0)).astype(BF16)
    slot_grads = (
        dot(carried, proj_weight, 1, 1)
        + dot(low_one, through_one_part, 0, 0)
        + dot(low_zero_part, through_zero, 1, 0)
    ).astype(BF16)

    target = slots_of_rows(row_owner, readers, per_peer)
    place = (lax.broadcasted_iota(jnp.int32, (slots, slots), 0) == target).astype(BF16)
    enc_part = lax.dynamic_slice_in_dim(enc_block, lax.axis_index("mp") * part, part, axis=1)
    routed = dot(place, enc_part, 1, 0).astype(BF16)

    back_blocks = slot_grads.reshape(readers, per_peer, feature_parts, part).transpose(0, 2, 1, 3)
    out_blocks = jnp.broadcast_to(
        routed.reshape(readers, 1, per_peer, part), (readers, feature_parts, per_peer, part)
    )
    blocks = jnp.concatenate([back_blocks, out_blocks], axis=3).reshape(readers * feature_parts, per_peer, 2 * part)
    blocks = lax.all_to_all(blocks, ("seq", "mp"), split_axis=0, concat_axis=0, tiled=True)
    blocks = blocks.reshape(readers, feature_parts, per_peer, 2 * part)
    returned = jnp.sum(blocks[..., :part].astype(F32), axis=1).astype(BF16).reshape(slots, part)
    returned = send_along(returned, "section", -2)
    arrived = blocks[..., part:].transpose(0, 2, 1, 3).reshape(slots, graph_width)
    soft_block = dot(arrived, proj_weight, 1, 0).astype(BF16)
    row_grads = dot(place, returned, 0, 0)
    return soft_block[None], row_grads[None]


def solution(mesh):
    placed = (
        P("section", "seq", None),
        P(None, "mp"),
        P("section", "seq"),
        P("section", "seq", "mp"),
        P("section", "mp"),
        P("section", None, "mp"),
        P("section", None, "mp"),
    )
    return jax.shard_map(
        on_device,
        mesh=mesh,
        in_specs=placed,
        out_specs=(P("section", "seq", "mp"), P("section", "seq", "mp")),
        check_vma=False,
    )
```

time: 206 us -> 92.1 us (0.45)
  waiting for transfers between devices: 86.1 us -> 2.23 us
  between operations: 14.2 us -> 0.88 us
  local copies, waits for them, and re-layouts: 11.1 us -> 1.78 us
  starting transfers between devices: 27.4 us -> 21.1 us
  matrix products: 12.5 us -> 17.7 us
  blocking collectives: 51.3 us -> 46.8 us
  other arithmetic: 3.16 us -> 0.24 us
    psum x3 -> x0, blocking collectives: 51.3 us -> none  [adapter_back(): reduced = lax.psum(partial_low, 'mp').astype(jnp.bfloat16)]
    ppermute x2 -> x5, waiting for transfers between devices: 42.8 us -> 2.23 us  [send_along(): lax.ppermute(value, axis, [(i, (i + steps) % count) for i in range(count)])]
    all_to_all x2 -> x0, waiting for transfers between devices: 35.4 us -> none  [the longest x1 20.7 us: on_device(): lax.all_to_all(outgoing, 'seq', split_axis=0, concat_axis=0, tiled=True)]
    all_to_all x0 -> x1, blocking collectives: none -> 27.5 us  [on_device(): lax.all_to_all(blocks, ('seq', 'mp'), split_axis=0, concat_axis=0, tiled=...]
    all_gather x0 -> x2, blocking collectives: none -> 19.3 us  [the longest x1 13.3 us: on_device(): lax.all_gather(first, 'mp').astype(F32)]
    all_to_all x2 -> x0, starting transfers between devices: 16.3 us -> none  [the longest x1 9.05 us: on_device(): lax.all_to_all(carried, 'seq', split_axis=0, concat_axis=0, tiled=True)]
    ppermute x2 -> x5, starting transfers between devices: 11 us -> 21.1 us  [send_along(): lax.ppermute(value, axis, [(i, (i + steps) % count) for i in range(count)])]
    reduce_scatter x1 -> x0, waiting for transfers between devices: 7.92 us -> none  [on_device(): lax.psum_scatter(partial_rows, 'mp', scatter_dimension=1, tiled=True)]
  transfers between devices with their start and end apart: 5 -> 5, of which waited for: 5 -> 1; matrix products, arithmetic and copies ran while one was open for 8% -> 18% of each run, Pallas kernels for 0% -> 0%
where the time goes in v1:
time: 92.1 us; the launch traced here: 90.8 us
  blocking collectives  46.8 us (51%)
  starting transfers between devices  21.1 us (23%)
  matrix products  17.7 us (19%)
  waiting for transfers between devices  2.23 us (2%)
  local copies, waits for them, and re-layouts  1.78 us (2%)
    all_to_all x1, blocking collectives, on_device(): lax.all_to_all(blocks, ('seq', 'mp'), split_axis=0, concat_axis=0, tiled=...  27.5 us
    ppermute x5, starting transfers between devices, send_along(): lax.ppermute(value, axis, [(i, (i + steps) % count) for i in range(count)])  21.1 us
    dot_general x13, matrix products, dot(): lax.dot_general(a, b, (((contract_a,), (contract_b,)), ((), ())), preferr...  17.7 us
    all_gather x1, blocking collectives, on_device(): lax.all_gather(first, 'mp').astype(F32)  13.3 us
    all_gather x1, blocking collectives, on_device(): lax.all_gather(low_one_part, 'mp').astype(F32)  5.98 us
    ppermute x5, waiting for transfers between devices, send_along(): lax.ppermute(value, axis, [(i, (i + steps) % count) for i in range(count)])  2.23 us
  transfers between devices with their start and end apart: 5, of which 1 were waited for; matrix products, arithmetic and copies ran while one was open for 18% of the time, Pallas kernels for 0%

profile of v1, /device:TPU:1, one launch (start us, length us, event | category | flops | bytes accessed | tf_op | source)
XLA Modules:
  0.0 90.8 jit_solution(10448411957463597653)
XLA Ops:
  0.6 0.0 copy-start
  0.6 5.0 %collective-permute-start = (bf16[64,2048]{1,0:T(8,128)(2,1)}, bf16[64,2048]{1,0:T(8,128)(2,1)}, u32[]{:S(2)}, u32[]{:S(2)}) collective-permute-start(bf16[64,2048]{1,0:T(8,128)(2,1)} %bitcast.60), channel_id=1, source_target_pairs={{0,4},{4,8},{8,12},{12,16},{16,20},{20,24},{24,28},{28,32},{32,36}... | collective-permute-start | bytes 786440 | tf_op jit(solution)/shard_map/ppermute | solution.py:12
  5.6 5.8 %collective-permute-start.2 = (bf16[64,2048]{1,0:T(8,128)(2,1)}, bf16[64,2048]{1,0:T(8,128)(2,1)}, u32[]{:S(2)}, u32[]{:S(2)}) collective-permute-start(bf16[64,2048]{1,0:T(8,128)(2,1)} %bitcast.61), channel_id=1, source_target_pairs={{0,8},{4,12},{8,16},{12,20},{16,24},{20,28},{24,32},{28,36},{32,40... | collective-permute-start | bytes 786440 | tf_op jit(solution)/shard_map/ppermute | solution.py:12
  11.4 1.8 %convolution_convert_fusion.4 = bf16[64,256]{1,0:T(8,128)(2,1)S(1)} fusion(bf16[1,256,2048]{2,1,0:T(8,128)(2,1)} %param.10, bf16[1,64,2048]{2,1,0:T(8,128)(2,1)} %param.13), kind=kOutput, calls=%fused_computation.13 | convolution fusion | flops 67125248 | bytes 1343488 | tf_op jit(solution)/shard_map/dot_general | solution.py:16
  13.2 0.0 copy-start.1
  13.2 0.0 copy-start.3
  13.2 0.0 copy-done
  13.2 1.8 %convolution_convert_fusion.1 = bf16[64,512]{1,0:T(8,128)(2,1)S(1)} fusion(bf16[512,2048]{1,0:T(8,128)(2,1)S(1)} %copy-done, bf16[1,64,2048]{2,1,0:T(8,128)(2,1)} %param.12, f32[2048]{0:T(1024)} %bitcast.64), kind=kOutput, calls=%fused_computation.10 | convolution fusion | flops 134643712 | bytes 2433024 | tf_op jit(solution)/shard_map/dot_general | solution.py:16
  15.0 13.3 %all-gather = bf16[256,768]{1,0:T(8,128)(2,1)S(1)} all-gather(bf16[64,768]{1,0:T(8,128)(2,1)S(1)} %pad_maximum_fusion.1), channel_id=2, replica_groups=mesh['seq'=16,'section'=16,'mp'=4] {'mp'}, dimensions={0}, use_global_device_ids=true | all-gather | bytes 491520 | tf_op jit(solution)/shard_map/all_gather | solution.py:50
  28.3 0.1 reduce_sum.45
  28.4 0.0 copy-start.2
  28.4 0.6 slice.27
  29.1 0.0 copy-done.2
  29.1 1.9 %collective-permute-start.3 = (bf16[64,512]{1,0:T(8,128)(2,1)}, bf16[64,512]{1,0:T(8,128)(2,1)}, u32[]{:S(2)}, u32[]{:S(2)}) collective-permute-start(bf16[64,512]{1,0:T(8,128)(2,1)} %slice.27), channel_id=1, source_target_pairs={{0,8},{4,12},{8,16},{12,20},{16,24},{20,28},{24,32},{28,36},{32,40... | collective-permute-start | bytes 196616 | tf_op jit(solution)/shard_map/ppermute | solution.py:12
  31.0 0.0 copy-done.1
  31.0 0.0 copy-done.3
  31.0 1.7 %fusion = bf16[256,2048]{1,0:T(8,128)(2,1)S(1)} fusion(bf16[1,256,2048]{2,1,0:T(8,128)(2,1)} %param.10, bf16[1,64,2048]{2,1,0:T(8,128)(2,1)S(1)} %copy-done.1, f32[2048]{0:T(1024)S(1)} %bitcast.65, bf16[64,768]{1,0:T(8,128)(2,1)} %copy-done.2), kind=kOutput, calls=%fused_computation.1 | convolution fusion | flops 69074944 | bytes 2400256 | tf_op jit(solution)/shard_map/dot_general | solution.py:16
  32.7 0.0 copy-start.6
  32.7 1.5 %fusion.24 = f32[256,512]{1,0:T(8,128)} fusion(bf16[256,2048]{1,0:T(8,128)(2,1)S(1)} %fusion, bf16[512,2048]{1,0:T(8,128)(2,1)S(1)} %copy-done), kind=kOutput, calls=%fused_computation.43 | convolution fusion | flops 536870912 | bytes 3670016 | tf_op jit(solution)/shard_map/dot_general | solution.py:16
  34.3 0.0 copy-done.6
  34.3 0.2 fusion.5
  34.4 0.0 copy-start.4
  34.5 1.7 %convolution_convert_fusion.2 = bf16[256,128]{1,0:T(8,128)(2,1)} fusion(s32[256]{0:T(256)S(1)} %bitcast.67, bf16[1,256,512]{2,1,0:T(8,128)(2,1)} %param.7, s32[]{:T(128)S(6)} %select_n.13), kind=kOutput, calls=%fused_computation.11 | convolution fusion | flops 16875520 | bytes 132100 | tf_op jit(solution)/shard_map/dot_general | solution.py:16
  36.1 0.0 collective-permute-done
  36.1 0.0 copy-done.4
  36.1 1.2 %convolution_convert_fusion.5 = bf16[64,64]{1,0:T(8,128)(2,1)S(1)} fusion(bf16[64,2048]{1,0:T(8,128)(2,1)} %collective-permute-done, bf16[1,64,2048]{2,1,0:T(8,128)(2,1)S(1)} %copy-done.1, f32[2048]{0:T(1024)S(1)} %bitcast.66), kind=kOutput, calls=%fused_computation.15 | convolution fusion | flops 17174528 | bytes 540672 | tf_op jit(solution)/shard_map/dot_general | solution.py:16
  37.3 3.3 %collective-permute-start.1 = (bf16[64,576]{1,0:T(8,128)(2,1)S(1)}, bf16[64,576]{1,0:T(8,128)(2,1)S(1)}, u32[]{:S(2)}, u32[]{:S(2)}) collective-permute-start(bf16[64,576]{1,0:T(8,128)(2,1)S(1)} %pad_maximum_fusion.2), channel_id=1, source_target_pairs={{0,4},{4,8},{8,12},{12,16},{16,20},{20,24},{24,28},{28,32},{32,36}... | collective-permute-start | bytes 221192 | tf_op jit(solution)/shard_map/ppermute | solution.py:12
  40.6 1.4 %fusion.4 = bf16[64,256]{1,0:T(8,128)(2,1)S(1)} fusion(bf16[256,2048]{1,0:T(8,128)(2,1)S(1)} %fusion, bf16[64,2048]{1,0:T(8,128)(2,1)} %collective-permute-done), kind=kOutput, calls=%fused_computation.14 | convolution fusion | flops 67125248 | bytes 1343488 | tf_op jit(solution)/shard_map/dot_general | solution.py:16
  42.0 6.0 %all-gather.1 = bf16[256,256]{1,0:T(8,128)(2,1)S(1)} all-gather(bf16[64,256]{1,0:T(8,128)(2,1)S(1)} %fusion.4), channel_id=3, replica_groups=mesh['seq'=16,'section'=16,'mp'=4] {'mp'}, dimensions={0}, use_global_device_ids=true | all-gather | bytes 163840 | tf_op jit(solution)/shard_map/all_gather | solution.py:58
  48.0 0.0 collective-permute-done.1
  48.0 2.1 %convolution_add_fusion.2 = f32[256,512]{1,0:T(8,128)} fusion(f32[256,512]{1,0:T(8,128)} %fusion.24, bf16[64,256]{1,0:T(8,128)(2,1)S(1)} %reduce_sum.46, bf16[64,576]{1,0:T(8,128)(2,1)S(1)} %collective-permute-done.1), kind=kOutput, calls=%fused_computation.5 | convolution fusion | flops 16908288 | bytes 1146880 | tf_op jit(solution)/shard_map/dot_general | solution.py:16
  50.1 0.2 fusion.19
  50.3 0.0 collective-permute-done.3
  50.3 0.0 collective-permute-done.2
  50.3 1.7 %fusion.2 = bf16[256,512]{1,0:T(8,128)(2,1)S(1)} fusion(f32[256,512]{1,0:T(8,128)} %convolution_add_fusion.2, bf16[64,512]{1,0:T(8,128)(2,1)} %collective-permute-done.3, f32[256,64]{1,0:T(8,128)S(1)} %fusion.19, bf16[256,2048]{1,0:T(8,128)(2,1)S(1)} %fusion, bf16[64,2048]{1,0:T(8,128)(2,1)} %collective-permute-done.2), kind=kOutput, calls=%fused_computation.6 | convolution fusion | flops 84180992 | bytes 2228224 | tf_op jit(solution)/shard_map/dot_general | solution.py:16
  52.1 0.1 reshape.33
  52.2 0.9 broadcast_in_dim.25
  53.1 0.1 pad_maximum_fusion
  53.1 27.5 %all_to_all.5 = bf16[64,16,256]{2,1,0:T(8,128)(2,1)S(1)} all-to-all(bf16[64,16,256]{2,1,0:T(8,128)(2,1)S(1)} %bitcast.55), channel_id=1, replica_groups=mesh['seq'=16,'section'=16,'mp'=4] {'seq','mp'}, dimensions={0} | all-to-all | bytes 1048576 | tf_op jit(solution)/shard_map/all_to_all | solution.py:77
  80.6 0.1 slice_reduce_fusion
  80.7 0.0 copy-start.5
  80.7 5.1 %collective-permute-start.4 = (bf16[256,128]{1,0:T(8,128)(2,1)S(1)}, bf16[256,128]{1,0:T(8,128)(2,1)S(1)}, u32[]{:S(2)}, u32[]{:S(2)}) collective-permute-start(bf16[256,128]{1,0:T(8,128)(2,1)S(1)} %bitcast.63), channel_id=1, source_target_pairs={{0,56},{4,60},{8,0},{12,4},{16,8},{20,12},{24,16},{28,20},{32,24},... | collective-permute-start | bytes 196616 | tf_op jit(solution)/shard_map/ppermute | solution.py:12
  85.8 0.1 copy.11
  86.0 1.7 %fusion.1 = bf16[1,256,2048]{2,1,0:T(8,128)(2,1)} fusion(bf16[512,2048]{1,0:T(8,128)(2,1)S(1)} %copy-done, bf16[32,8,4,128]{3,2,1,0:T(4,128)(2,1)S(1)} %bitcast.58), kind=kOutput, calls=%fused_computation.3 | convolution fusion | flops 537395200 | bytes 3407872 | tf_op jit(solution)/shard_map/dot_general | solution.py:16
  87.7 2.2 %collective-permute-done.4 = bf16[256,128]{1,0:T(8,128)(2,1)S(1)} collective-permute-done((bf16[256,128]{1,0:T(8,128)(2,1)S(1)}, bf16[256,128]{1,0:T(8,128)(2,1)S(1)}, u32[]{:S(2)}, u32[]{:S(2)}) %collective-permute-start.4) | collective-permute-done | bytes 65568 | tf_op jit(solution)/shard_map/ppermute | solution.py:12
  89.9 0.0 copy-done.5
  89.9 0.9 %convolution_bitcast_fusion = f32[1,256,128]{2,1,0:T(8,128)} fusion(bf16[256,128]{1,0:T(8,128)(2,1)S(1)} %collective-permute-done.4, s32[256]{0:T(256)S(1)} %bitcast.68), kind=kOutput, calls=%fused_computation.7 | convolution fusion | flops 16842752 | bytes 197632 | tf_op jit(solution)/shard_map/dot_general | solution.py:16
  (6 shorter events, 0.1 us)
Async XLA Ops:
  0.6 12.6 %copy-start = (bf16[512,2048]{1,0:T(8,128)(2,1)S(1)}, bf16[512,2048]{1,0:T(8,128)(2,1)}, u32[]{:S(2)}) copy-start(bf16[512,2048]{1,0:T(8,128)(2,1)} %param.8) | copy-start | bytes 6291460
  0.6 35.5 %collective-permute-start = (bf16[64,2048]{1,0:T(8,128)(2,1)}, bf16[64,2048]{1,0:T(8,128)(2,1)}, u32[]{:S(2)}, u32[]{:S(2)}) collective-permute-start(bf16[64,2048]{1,0:T(8,128)(2,1)} %bitcast.60), channel_id=1, source_target_pairs={{0,4},{4,8},{8,12},{12,16},{16,20},{20,24},{24,28},{28,32},{32,36}... | collective-permute-start | bytes 786440 | tf_op jit(solution)/shard_map/ppermute | solution.py:12
  5.6 44.7 %collective-permute-start.2 = (bf16[64,2048]{1,0:T(8,128)(2,1)}, bf16[64,2048]{1,0:T(8,128)(2,1)}, u32[]{:S(2)}, u32[]{:S(2)}) collective-permute-start(bf16[64,2048]{1,0:T(8,128)(2,1)} %bitcast.61), channel_id=1, source_target_pairs={{0,8},{4,12},{8,16},{12,20},{16,24},{20,28},{24,32},{28,36},{32,40... | collective-permute-start | bytes 786440 | tf_op jit(solution)/shard_map/ppermute | solution.py:12
  13.2 17.8 %copy-start.1 = (bf16[1,64,2048]{2,1,0:T(8,128)(2,1)S(1)}, bf16[1,64,2048]{2,1,0:T(8,128)(2,1)}, u32[]{:S(2)}) copy-start(bf16[1,64,2048]{2,1,0:T(8,128)(2,1)} %param.12) | copy-start | bytes 786436
  13.2 17.8 %copy-start.3 = (f32[1,2048]{1,0:T(1,128)S(1)}, f32[1,2048]{1,0:T(1,128)}, u32[]{:S(2)}) copy-start(f32[1,2048]{1,0:T(1,128)} %param.11) | copy-start | bytes 24580
  28.4 0.7 copy-start.2
  29.1 21.3 %collective-permute-start.3 = (bf16[64,512]{1,0:T(8,128)(2,1)}, bf16[64,512]{1,0:T(8,128)(2,1)}, u32[]{:S(2)}, u32[]{:S(2)}) collective-permute-start(bf16[64,512]{1,0:T(8,128)(2,1)} %slice.27), channel_id=1, source_target_pairs={{0,8},{4,12},{8,16},{12,20},{16,24},{20,28},{24,32},{28,36},{32,40... | collective-permute-start | bytes 196616 | tf_op jit(solution)/shard_map/ppermute | solution.py:12
  32.7 1.6 %copy-start.6 = (s32[1,256]{1,0:T(1,128)S(1)}, s32[1,256]{1,0:T(1,128)}, u32[]{:S(2)}) copy-start(s32[1,256]{1,0:T(1,128)} %param.9) | copy-start | bytes 3076
  34.4 1.7 %copy-start.4 = (s32[1,256]{1,0:T(1,128)}, s32[1,256]{1,0:T(1,128)S(1)}, u32[]{:S(2)}) copy-start(s32[1,256]{1,0:T(1,128)S(1)} %compare_select_fusion) | copy-start | bytes 3076
  37.3 10.7 %collective-permute-start.1 = (bf16[64,576]{1,0:T(8,128)(2,1)S(1)}, bf16[64,576]{1,0:T(8,128)(2,1)S(1)}, u32[]{:S(2)}, u32[]{:S(2)}) collective-permute-start(bf16[64,576]{1,0:T(8,128)(2,1)S(1)} %pad_maximum_fusion.2), channel_id=1, source_target_pairs={{0,4},{4,8},{8,12},{12,16},{16,20},{20,24},{24,28},{28,32},{32,36}... | collective-permute-start | bytes 221192 | tf_op jit(solution)/shard_map/ppermute | solution.py:12
  80.7 9.2 %copy-start.5 = (s32[1,256]{1,0:T(1,128)S(1)}, s32[1,256]{1,0:T(1,128)}, u32[]{:S(2)}) copy-start(s32[1,256]{1,0:T(1,128)} %copy-done.4) | copy-start | bytes 3076
  80.7 9.2 %collective-permute-start.4 = (bf16[256,128]{1,0:T(8,128)(2,1)S(1)}, bf16[256,128]{1,0:T(8,128)(2,1)S(1)}, u32[]{:S(2)}, u32[]{:S(2)}) collective-permute-start(bf16[256,128]{1,0:T(8,128)(2,1)S(1)} %bitcast.63), channel_id=1, source_target_pairs={{0,56},{4,60},{8,0},{12,4},{16,8},{20,12},{24,16},{28,20},{32,24},... | collective-permute-start | bytes 196616 | tf_op jit(solution)/shard_map/ppermute | solution.py:12

commit v2 on v1

v2 whole, which is shorter than its diff:
```python
import functools

import jax
import jax.numpy as jnp
from jax import lax
from jax.experimental import pallas as pl
from jax.experimental.pallas import tpu as pltpu
from jax.sharding import PartitionSpec as P

BF16 = jnp.bfloat16
F32 = jnp.float32


def send_along(value, axis, steps):
    count = lax.axis_size(axis)
    return lax.ppermute(value, axis, [(i, (i + steps) % count) for i in range(count)])


def dot(a, b, contract_a, contract_b):
    return lax.dot_general(a, b, (((contract_a,), (contract_b,)), ((), ())), preferred_element_type=F32)


def call_kernel(body, outs, *args):
    return pl.pallas_call(
        body,
        out_shape=[jax.ShapeDtypeStruct(shape, kind) for shape, kind in outs],
        in_specs=[pl.BlockSpec(memory_space=pltpu.VMEM)] * len(args),
        out_specs=[pl.BlockSpec(memory_space=pltpu.VMEM)] * len(outs),
        compiler_params=pltpu.CompilerParams(vmem_limit_bytes=24 << 20),
    )(*args)


def slots_of_rows(owners, readers, per_peer):
    rows = owners.shape[1]
    reader = lax.broadcasted_iota(jnp.int32, (readers, rows), 0)
    is_owner = reader == owners
    matches = jnp.where(is_owner, 1.0, 0.0).astype(BF16)
    earlier = lax.broadcasted_iota(jnp.int32, (rows, rows), 0) < lax.broadcasted_iota(jnp.int32, (rows, rows), 1)
    before = dot(matches, jnp.where(earlier, 1.0, 0.0).astype(BF16), 1, 0)
    rank = jnp.sum(jnp.where(is_owner, before, 0.0), axis=0, keepdims=True).astype(jnp.int32)
    return jnp.where(owners >= 0, owners * per_peer + rank, -1)


def relay_kernel(gathered_ref, first_ref, up_one_ref, scaled_ref, onward_ref, through_ref, low_two_ref):
    slots = low_two_ref.shape[1]
    rank, features = up_one_ref.shape
    width = through_ref.shape[1]
    onward_ref[:, :features] = up_one_ref[...]
    onward_ref[:, features : features + width] = first_ref[:, slots:]
    cross = dot(scaled_ref[...], up_one_ref[...], 1, 1).astype(BF16)
    onward_ref[:, features + width :] = jnp.concatenate([cross, jnp.zeros_like(cross)], axis=1)
    total = jnp.sum(gathered_ref[...].astype(F32), axis=0)
    low_two_ref[...] = total[:, :slots].astype(BF16)
    through_ref[...] = total[:, slots:].astype(BF16)


def carry_kernel(readers, owner_ref, enc_ref, grad_ref, low_two_ref, scaled_ref, up_one_ref, weight_ref,
                 carried_ref, low_one_ref, direct_ref, target_ref, routed_ref):
    slots = grad_ref.shape[0]
    low_two = low_two_ref[...].astype(F32).T.astype(BF16)
    carried = (grad_ref[...].astype(F32) + dot(low_two, scaled_ref[...], 1, 0)).astype(BF16)
    carried_ref[...] = carried
    low_one_ref[...] = dot(up_one_ref[...], carried, 1, 1).astype(BF16)
    direct_ref[...] = dot(carried, weight_ref[...], 1, 1)
    target = slots_of_rows(owner_ref[...], readers, slots // readers)
    target_ref[...] = target
    is_place = lax.broadcasted_iota(jnp.int32, (slots, slots), 0) == target
    place = jnp.where(is_place, 1.0, 0.0).astype(BF16)
    part = routed_ref.shape[1]
    mine = pl.multiple_of(lax.axis_index("mp") * part, part)
    routed_ref[...] = dot(place, enc_ref[:, pl.ds(mine, part)], 1, 0).astype(BF16)


def finish_kernel(gathered_ref, onward_ref, through_zero_ref, carried_ref, direct_ref, routed_ref, blocks_ref):
    features = carried_ref.shape[1]
    width = direct_ref.shape[1]
    rank = onward_ref.shape[0]
    readers, parts, rows, part = blocks_ref.shape
    pair = rows // 3
    low_one = jnp.sum(gathered_ref[...].astype(F32), axis=0)
    cross = onward_ref[:, features + width :].astype(F32)[:, :rank].T.astype(BF16)
    low_zero = dot(onward_ref[:, :features], carried_ref[...], 1, 1) + dot(cross, low_one.astype(BF16), 1, 0)
    lows = jnp.concatenate([low_one, low_zero], axis=0).T.astype(BF16)
    throughs = jnp.concatenate([onward_ref[:, features : features + width], through_zero_ref[...]], axis=0)
    slot_grads = direct_ref[...] + dot(lows, throughs, 1, 0)
    routed = routed_ref[...].astype(F32).reshape(readers, 2 * pair, part)
    for i in range(parts):
        block = slot_grads[:, i * part : (i + 1) * part].reshape(readers, 2 * pair, part)
        half = routed[:, (i % 2) * pair : (i % 2 + 1) * pair]
        blocks_ref[:, i] = jnp.concatenate([block, half], axis=1).astype(BF16)


def on_device(enc_rows, proj_weight, row_owner, grad_in, adapter_gain, adapter_down, adapter_up):
    readers = lax.axis_size("seq")
    feature_parts = lax.axis_size("mp")
    enc_block, grad, up, down = enc_rows[0], grad_in[0], adapter_up[0], adapter_down[0]
    slots = grad.shape[0]
    rank, features = up.shape
    per_peer = slots // readers
    width = enc_block.shape[1]
    part = width // feature_parts
    pair = per_peer // 2

    up_one = send_along(up, "section", 1)
    scaled = (down.astype(F32) * adapter_gain).astype(BF16)
    first = jnp.concatenate([dot(up, grad, 1, 1).astype(BF16), dot(scaled, proj_weight, 1, 1).astype(BF16)], axis=1)
    gathered = lax.all_gather(first, "mp")
    onward, through, low_two = call_kernel(
        relay_kernel,
        [((rank, features + width + 2 * rank), BF16), ((rank, width), BF16), ((rank, slots), BF16)],
        gathered, first, up_one, scaled,
    )
    onward = send_along(onward, "section", 1)
    through_zero = send_along(through, "section", 2)
    carried, low_one, direct, target, routed = call_kernel(
        functools.partial(carry_kernel, readers),
        [((slots, features), BF16), ((rank, slots), BF16), ((slots, width), F32), ((1, slots), jnp.int32), ((slots, part), BF16)],
        row_owner, enc_block, grad, low_two, scaled, up_one, proj_weight,
    )
    gathered = lax.all_gather(low_one, "mp")
    (blocks,) = call_kernel(
        finish_kernel,
        [((readers, feature_parts, per_peer + pair, part), BF16)],
        gathered, onward, through_zero, carried, direct, routed,
    )
    blocks = blocks.reshape(readers * feature_parts, per_peer + pair, part)
    blocks = lax.all_to_all(blocks, ("seq", "mp"), split_axis=0, concat_axis=0, tiled=True)
    blocks = blocks.reshape(readers, feature_parts, per_peer + pair, part)
    returned = jnp.sum(blocks[:, :, :per_peer].astype(F32), axis=1).astype(BF16).reshape(slots, part)
    returned = send_along(returned, "section", -2)
    own_half = blocks[:, :, per_peer:]
    other_half = lax.ppermute(own_half, "mp", [(i, i ^ 1) for i in range(feature_parts)])
    is_even = lax.axis_index("mp") % 2 == 0
    arrived = jnp.stack(
        [jnp.where(is_even, own_half, other_half), jnp.where(is_even, other_half, own_half)], axis=1
    )
    arrived = arrived.transpose(0, 1, 3, 2, 4).reshape(slots, width)
    soft_block = dot(arrived, proj_weight, 1, 0).astype(BF16)
    place = (lax.broadcasted_iota(jnp.int32, (slots, slots), 0) == target).astype(BF16)
    row_grads = dot(place, returned, 0, 0)
    return soft_block[None], row_grads[None]


def solution(mesh):
    placed = (
        P("section", "seq", None),
        P(None, "mp"),
        P("section", "seq"),
        P("section", "seq", "mp"),
        P("section", "mp"),
        P("section", None, "mp"),
        P("section", None, "mp"),
    )
    return jax.shard_map(
        on_device,
        mesh=mesh,
        in_specs=placed,
        out_specs=(P("section", "seq", "mp"), P("section", "seq", "mp")),
        check_vma=False,
    )
```

time: 92.1 us -> 81.2 us (0.88); the launches traced: 90.8 us -> 80.8 us
  matrix products: 17.7 us -> 5.4 us
  starting transfers between devices: 21.1 us -> 14.9 us
  waiting for transfers between devices: 2.23 us -> 7.76 us
  Pallas kernels: 0 us -> 2.6 us
  local copies, waits for them, and re-layouts: 1.78 us -> 0.05 us
  blocking collectives: 46.8 us -> 48.2 us
    dot_general x13 -> x4, matrix products: 17.7 us -> 5.4 us  [dot(): lax.dot_general(a, b, (((contract_a,), (contract_b,)), ((), ())), preferr...]
    ppermute x5 -> x4, starting transfers between devices: 21.1 us -> 12.5 us  [send_along(): lax.ppermute(value, axis, [(i, (i + steps) % count) for i in range(count)])]
    ppermute x5 -> x4, waiting for transfers between devices: 2.23 us -> 7.75 us  [send_along(): lax.ppermute(value, axis, [(i, (i + steps) % count) for i in range(count)])]
    all_gather x2, blocking collectives: 19.3 us -> 22.8 us  [the longest x1 17.4 us: on_device(): gathered = lax.all_gather(first, 'mp')]
    pallas_call x0 -> x3, Pallas kernels: none -> 2.6 us  [call_kernel(): pl.pallas_call(body, out_shape=[jax.ShapeDtypeStruct(shape, kind) for sha...]
    ppermute x0 -> x1, starting transfers between devices: none -> 2.46 us  [on_device(): lax.ppermute(own_half, 'mp', [(i, i ^ 1) for i in range(feature_parts)])]
    all_to_all x1, blocking collectives: 27.5 us -> 25.4 us  [on_device(): lax.all_to_all(blocks, ('seq', 'mp'), split_axis=0, concat_axis=0, tiled=...]
    convert_element_type x1, other arithmetic: 0.01 us -> 1 us  [on_device(): scaled = (down.astype(F32) * adapter_gain).astype(BF16)]
  transfers between devices with their start and end apart: 5 -> 5, of which waited for: 1 -> 2; matrix products, arithmetic and copies ran while one was open for 18% -> 6% of each run, Pallas kernels for 0% -> 2%
where the time goes in v2:
time: 81.2 us; the launch traced here: 80.8 us
  blocking collectives  48.2 us (59%)
  starting transfers between devices  14.9 us (18%)
  waiting for transfers between devices  7.76 us (10%)
  matrix products  5.4 us (7%)
  Pallas kernels  2.6 us (3%)
  other arithmetic  1.09 us (1%)
  between operations  0.82 us (1%)
    all_to_all x1, blocking collectives, on_device(): lax.all_to_all(blocks, ('seq', 'mp'), split_axis=0, concat_axis=0, tiled=...  25.4 us
    all_gather x1, blocking collectives, on_device(): gathered = lax.all_gather(first, 'mp')  17.4 us
    ppermute x4, starting transfers between devices, send_along(): lax.ppermute(value, axis, [(i, (i + steps) % count) for i in range(count)])  12.5 us
    ppermute x4, waiting for transfers between devices, send_along(): lax.ppermute(value, axis, [(i, (i + steps) % count) for i in range(count)])  7.75 us
    all_gather x1, blocking collectives, on_device(): gathered = lax.all_gather(low_one, 'mp')  5.42 us
    dot_general x4, matrix products, dot(): lax.dot_general(a, b, (((contract_a,), (contract_b,)), ((), ())), preferr...  5.4 us
    pallas_call x3, Pallas kernels, call_kernel(): pl.pallas_call(body, out_shape=[jax.ShapeDtypeStruct(shape, kind) for sha...  2.6 us
    ppermute x1, starting transfers between devices, on_device(): lax.ppermute(own_half, 'mp', [(i, i ^ 1) for i in range(feature_parts)])  2.46 us
  transfers between devices with their start and end apart: 5, of which 2 were waited for; matrix products, arithmetic and copies ran while one was open for 6% of the time, Pallas kernels for 2%

profile of v2, /device:TPU:1, one launch (start us, length us, event | category | flops | bytes accessed | tf_op | source)
XLA Modules:
  0.0 80.8 jit_solution(1545635840422077341)
XLA Ops:
  0.6 0.0 copy-start.4
  0.6 0.0 copy-start.1
  0.7 5.0 %collective-permute-start = (bf16[64,2048]{1,0:T(8,128)(2,1)}, bf16[64,2048]{1,0:T(8,128)(2,1)S(1)}, u32[]{:S(2)}, u32[]{:S(2)}) collective-permute-start(bf16[64,2048]{1,0:T(8,128)(2,1)} %bitcast.45), channel_id=1, source_target_pairs={{0,4},{4,8},{8,12},{12,16},{16,20},{20,24},{24,28},{28,32},{32,36}... | collective-permute-start | bytes 786440 | tf_op jit(solution)/shard_map/ppermute | solution.py:16
  5.6 1.0 %fusion.1.scaled_ref = bf16[64,2048]{1,0:T(8,128)(2,1)S(1)} fusion(bf16[1,64,2048]{2,1,0:T(8,128)(2,1)} %param.12, f32[2048]{0:T(1024)} %bitcast.47), kind=kLoop, calls=%fused_computation.6 | loop fusion | flops 393216 | bytes 532480 | tf_op jit(solution)/shard_map/convert_element_type | solution.py:105
  6.6 2.3 %convolution_convert_fusion.1 = bf16[64,512]{1,0:T(8,128)(2,1)S(1)} fusion(bf16[64,2048]{1,0:T(8,128)(2,1)S(1)} %fusion.1.scaled_ref, bf16[512,2048]{1,0:T(8,128)(2,1)} %weight_ref.1), kind=kOutput, calls=%fused_computation.3 | convolution fusion | flops 134250496 | bytes 2424832 | tf_op jit(solution)/shard_map/dot_general | solution.py:20
  9.0 0.0 copy-done.4
  9.0 0.0 copy-done.1
  9.0 0.0 copy-start
  9.0 0.0 copy-start.2
  9.0 0.0 copy-start.3
  9.0 0.4 convolution_convert_fusion.2
  9.5 17.4 %all-gather = bf16[256,768]{1,0:T(8,128)(2,1)S(1)} all-gather(bf16[64,768]{1,0:T(8,128)(2,1)S(1)} %pad_maximum_fusion.1.first_ref), channel_id=2, replica_groups=mesh['seq'=16,'section'=16,'mp'=4] {'mp'}, dimensions={0}, use_global_device_ids=true | all-gather | bytes 491520 | tf_op jit(solution)/shard_map/all_gather | solution.py:107
  26.9 0.0 collective-permute-done.up_one_ref
  26.9 0.2 shard_map.86
  27.1 1.9 %collective-permute-start.1 = (bf16[64,2688]{1,0:T(8,128)(2,1)S(1)}, bf16[64,2688]{1,0:T(8,128)(2,1)S(1)}, u32[]{:S(2)}, u32[]{:S(2)}) collective-permute-start(bf16[64,2688]{1,0:T(8,128)(2,1)S(1)} %get-tuple-element.12), channel_id=1, source_target_pairs={{0,4},{4,8},{8,12},{12,16},{16,20},{20,24},{24,28},{28,32},{32,36}... | collective-permute-start | bytes 1032200 | tf_op jit(solution)/shard_map/ppermute | solution.py:16
  29.0 1.9 %collective-permute-start.2 = (bf16[64,512]{1,0:T(8,128)(2,1)S(1)}, bf16[64,512]{1,0:T(8,128)(2,1)S(1)}, u32[]{:S(2)}, u32[]{:S(2)}) collective-permute-start(bf16[64,512]{1,0:T(8,128)(2,1)S(1)} %get-tuple-element.13), channel_id=1, source_target_pairs={{0,8},{4,12},{8,16},{12,20},{16,24},{20,28},{24,32},{28,36},{32,40... | collective-permute-start | bytes 196616 | tf_op jit(solution)/shard_map/ppermute | solution.py:16
  30.9 0.0 copy-done
  31.0 0.0 copy-done.2
  31.0 0.0 copy-done.3
  31.0 1.5 %shard_map.87 = (bf16[256,2048]{1,0:T(8,128)(2,1)S(1)}, bf16[64,256]{1,0:T(8,128)(2,1)S(1)}, f32[256,512]{1,0:T(8,128)S(1)}, s32[1,256]{1,0:T(1,128)S(1)}, bf16[256,128]{1,0:T(8,128)(2,1)S(1)}) custom-call(s32[1,256]{1,0:T(1,128)S(1)} %copy-done.3, bf16[256,512]{1,0:T(8,128)(2,1)S(1)} %bitcast.39, bf16[256,2048]{1,0:T(8,128)(2,1)S(1)} %bitcast.35, ...), custom_call_target="tpu_custom_call" | custom-call | tf_op jit(solution)/shard_map/pallas_call | solution.py:24
  32.5 5.4 %all-gather.1 = bf16[256,256]{1,0:T(8,128)(2,1)S(1)} all-gather(bf16[64,256]{1,0:T(8,128)(2,1)S(1)} %get-tuple-element.11), channel_id=3, replica_groups=mesh['seq'=16,'section'=16,'mp'=4] {'mp'}, dimensions={0}, use_global_device_ids=true | all-gather | bytes 163840 | tf_op jit(solution)/shard_map/all_gather | solution.py:120
  37.9 6.2 %collective-permute-done.2.through_zero_ref = bf16[64,512]{1,0:T(8,128)(2,1)S(1)} collective-permute-done((bf16[64,512]{1,0:T(8,128)(2,1)S(1)}, bf16[64,512]{1,0:T(8,128)(2,1)S(1)}, u32[]{:S(2)}, u32[]{:S(2)}) %collective-permute-start.2) | collective-permute-done | bytes 65568 | tf_op jit(solution)/shard_map/ppermute | solution.py:16
  44.1 0.0 collective-permute-done.1.onward_ref
  44.1 0.9 %shard_map.88 = bf16[16,4,24,128]{3,2,1,0:T(8,128)(2,1)S(1)} custom-call(bf16[4,64,256]{2,1,0:T(8,128)(2,1)S(1)} %bitcast.38, bf16[64,2688]{1,0:T(8,128)(2,1)S(1)} %collective-permute-done.1.onward_ref, bf16[64,512]{1,0:T(8,128)(2,1)S(1)} %collective-permute-done.2.through_zero_ref, bf16[256,2048]{1,0:T(8,128)(2,1)S(1)} %get-tuple-element.14.carried_ref, ...), custom_call_target="tpu_custom_call" | custom-call | tf_op jit(solution)/shard_map/pallas_call | solution.py:24
  45.0 25.4 %all_to_all.5 = bf16[64,24,128]{2,1,0:T(8,128)(2,1)S(1)} all-to-all(bf16[64,24,128]{2,1,0:T(8,128)(2,1)S(1)} %bitcast.36), channel_id=1, replica_groups=mesh['seq'=16,'section'=16,'mp'=4] {'seq','mp'}, dimensions={0} | all-to-all | bytes 786432 | tf_op jit(solution)/shard_map/all_to_all | solution.py:127
  70.4 3.7 %collective-permute-start.4 = (bf16[256,128]{1,0:T(8,128)(2,1)S(1)}, bf16[256,128]{1,0:T(8,128)(2,1)S(1)}, u32[]{:S(2)}, u32[]{:S(2)}) collective-permute-start(bf16[256,128]{1,0:T(8,128)(2,1)S(1)} %bitcast.46), channel_id=1, source_target_pairs={{0,56},{4,60},{8,0},{12,4},{16,8},{20,12},{24,16},{28,20},{32,24},... | collective-permute-start | bytes 196616 | tf_op jit(solution)/shard_map/ppermute | solution.py:16
  74.1 2.5 %collective-permute-start.3 = (bf16[16,4,8,128]{3,2,1,0:T(8,128)(2,1)S(1)}, bf16[16,4,8,128]{3,2,1,0:T(8,128)(2,1)S(1)}, u32[]{:S(2)}, u32[]{:S(2)}) collective-permute-start(bf16[16,4,8,128]{3,2,1,0:T(8,128)(2,1)S(1)} %slice.8), channel_id=1, source_target_pairs={{0,1},{1,0},{2,3},{3,2},{4,5},{5,4},{6,7},{7,6},{8,9},{9,8},{10,11... | collective-permute-start | bytes 393224 | tf_op jit(solution)/shard_map/ppermute | solution.py:132
  76.6 1.6 %collective-permute-done.4 = bf16[256,128]{1,0:T(8,128)(2,1)S(1)} collective-permute-done((bf16[256,128]{1,0:T(8,128)(2,1)S(1)}, bf16[256,128]{1,0:T(8,128)(2,1)S(1)}, u32[]{:S(2)}, u32[]{:S(2)}) %collective-permute-start.4) | collective-permute-done | bytes 65568 | tf_op jit(solution)/shard_map/ppermute | solution.py:16
  78.2 0.9 %convolution_bitcast_fusion = f32[1,256,128]{2,1,0:T(8,128)} fusion(bf16[256,128]{1,0:T(8,128)(2,1)S(1)} %collective-permute-done.4, s32[256]{0:T(256)S(1)} %bitcast.40), kind=kOutput, calls=%fused_computation.2 | convolution fusion | flops 16842752 | bytes 197632 | tf_op jit(solution)/shard_map/dot_general | solution.py:20
  79.1 0.0 collective-permute-done.3
  79.2 1.7 %fusion = bf16[1,256,2048]{2,1,0:T(8,128)(2,1)} fusion(bf16[256,512]{1,0:T(8,128)(2,1)S(1)} %bitcast.44, bf16[512,2048]{1,0:T(8,128)(2,1)S(1)} %copy-done), kind=kOutput, calls=%fused_computation.1 | convolution fusion | flops 537395200 | bytes 3407872 | tf_op jit(solution)/shard_map/dot_general | solution.py:20
  (5 shorter events, 0.1 us)
Async XLA Ops:
  0.6 8.3 %copy-start.4 = (bf16[1,64,2048]{2,1,0:T(8,128)(2,1)S(1)}, bf16[1,64,2048]{2,1,0:T(8,128)(2,1)}, u32[]{:S(2)}) copy-start(bf16[1,64,2048]{2,1,0:T(8,128)(2,1)} %param.13) | copy-start | bytes 786436
  0.6 8.3 %copy-start.1 = (bf16[1,256,2048]{2,1,0:T(8,128)(2,1)S(1)}, bf16[1,256,2048]{2,1,0:T(8,128)(2,1)}, u32[]{:S(2)}) copy-start(bf16[1,256,2048]{2,1,0:T(8,128)(2,1)} %param.10) | copy-start | bytes 3145732
  0.7 26.2 %collective-permute-start = (bf16[64,2048]{1,0:T(8,128)(2,1)}, bf16[64,2048]{1,0:T(8,128)(2,1)S(1)}, u32[]{:S(2)}, u32[]{:S(2)}) collective-permute-start(bf16[64,2048]{1,0:T(8,128)(2,1)} %bitcast.45), channel_id=1, source_target_pairs={{0,4},{4,8},{8,12},{12,16},{16,20},{20,24},{24,28},{28,32},{32,36}... | collective-permute-start | bytes 786440 | tf_op jit(solution)/shard_map/ppermute | solution.py:16
  9.0 22.0 %copy-start = (bf16[512,2048]{1,0:T(8,128)(2,1)S(1)}, bf16[512,2048]{1,0:T(8,128)(2,1)}, u32[]{:S(2)}) copy-start(bf16[512,2048]{1,0:T(8,128)(2,1)} %weight_ref.1) | copy-start | bytes 6291460
  9.0 21.9 %copy-start.2 = (bf16[1,256,512]{2,1,0:T(8,128)(2,1)S(1)}, bf16[1,256,512]{2,1,0:T(8,128)(2,1)}, u32[]{:S(2)}) copy-start(bf16[1,256,512]{2,1,0:T(8,128)(2,1)} %param.7) | copy-start | bytes 786436
  9.0 21.9 %copy-start.3 = (s32[1,256]{1,0:T(1,128)S(1)}, s32[1,256]{1,0:T(1,128)}, u32[]{:S(2)}) copy-start(s32[1,256]{1,0:T(1,128)} %owner_ref.1) | copy-start | bytes 3076
  27.1 17.0 %collective-permute-start.1 = (bf16[64,2688]{1,0:T(8,128)(2,1)S(1)}, bf16[64,2688]{1,0:T(8,128)(2,1)S(1)}, u32[]{:S(2)}, u32[]{:S(2)}) collective-permute-start(bf16[64,2688]{1,0:T(8,128)(2,1)S(1)} %get-tuple-element.12), channel_id=1, source_target_pairs={{0,4},{4,8},{8,12},{12,16},{16,20},{20,24},{24,28},{28,32},{32,36}... | collective-permute-start | bytes 1032200 | tf_op jit(solution)/shard_map/ppermute | solution.py:16
  29.0 15.1 %collective-permute-start.2 = (bf16[64,512]{1,0:T(8,128)(2,1)S(1)}, bf16[64,512]{1,0:T(8,128)(2,1)S(1)}, u32[]{:S(2)}, u32[]{:S(2)}) collective-permute-start(bf16[64,512]{1,0:T(8,128)(2,1)S(1)} %get-tuple-element.13), channel_id=1, source_target_pairs={{0,8},{4,12},{8,16},{12,20},{16,24},{20,28},{24,32},{28,36},{32,40... | collective-permute-start | bytes 196616 | tf_op jit(solution)/shard_map/ppermute | solution.py:16
  70.4 7.8 %collective-permute-start.4 = (bf16[256,128]{1,0:T(8,128)(2,1)S(1)}, bf16[256,128]{1,0:T(8,128)(2,1)S(1)}, u32[]{:S(2)}, u32[]{:S(2)}) collective-permute-start(bf16[256,128]{1,0:T(8,128)(2,1)S(1)} %bitcast.46), channel_id=1, source_target_pairs={{0,56},{4,60},{8,0},{12,4},{16,8},{20,12},{24,16},{28,20},{32,24},... | collective-permute-start | bytes 196616 | tf_op jit(solution)/shard_map/ppermute | solution.py:16
  74.1 5.0 %collective-permute-start.3 = (bf16[16,4,8,128]{3,2,1,0:T(8,128)(2,1)S(1)}, bf16[16,4,8,128]{3,2,1,0:T(8,128)(2,1)S(1)}, u32[]{:S(2)}, u32[]{:S(2)}) collective-permute-start(bf16[16,4,8,128]{3,2,1,0:T(8,128)(2,1)S(1)} %slice.8), channel_id=1, source_target_pairs={{0,1},{1,0},{2,3},{3,2},{4,5},{5,4},{6,7},{7,6},{8,9},{9,8},{10,11... | collective-permute-start | bytes 393224 | tf_op jit(solution)/shard_map/ppermute | solution.py:132

commit v3 on v2

--- a/solution.py
+++ b/solution.py
@@ -41,24 +41,28 @@
     return jnp.where(owners >= 0, owners * per_peer + rank, -1)
 
 
-def relay_kernel(gathered_ref, first_ref, up_one_ref, scaled_ref, onward_ref, through_ref, low_two_ref):
+def scaled_down(down_ref, gain_ref):
+    return (down_ref[...].astype(F32) * gain_ref[...]).astype(BF16)
+
+
+def relay_kernel(gathered_ref, first_ref, up_one_ref, down_ref, gain_ref, onward_ref, through_ref, low_two_ref):
     slots = low_two_ref.shape[1]
     rank, features = up_one_ref.shape
     width = through_ref.shape[1]
     onward_ref[:, :features] = up_one_ref[...]
     onward_ref[:, features : features + width] = first_ref[:, slots:]
-    cross = dot(scaled_ref[...], up_one_ref[...], 1, 1).astype(BF16)
+    cross = dot(scaled_down(down_ref, gain_ref), up_one_ref[...], 1, 1).astype(BF16)
     onward_ref[:, features + width :] = jnp.concatenate([cross, jnp.zeros_like(cross)], axis=1)
     total = jnp.sum(gathered_ref[...].astype(F32), axis=0)
     low_two_ref[...] = total[:, :slots].astype(BF16)
     through_ref[...] = total[:, slots:].astype(BF16)
 
 
-def carry_kernel(readers, owner_ref, enc_ref, grad_ref, low_two_ref, scaled_ref, up_one_ref, weight_ref,
+def carry_kernel(readers, owner_ref, enc_ref, grad_ref, low_two_ref, down_ref, gain_ref, up_one_ref, weight_ref,
                  carried_ref, low_one_ref, direct_ref, target_ref, routed_ref):
     slots = grad_ref.shape[0]
     low_two = low_two_ref[...].astype(F32).T.astype(BF16)
-    carried = (grad_ref[...].astype(F32) + dot(low_two, scaled_ref[...], 1, 0)).astype(BF16)
+    carried = (grad_ref[...].astype(F32) + dot(low_two, scaled_down(down_ref, gain_ref), 1, 0)).astype(BF16)
     carried_ref[...] = carried
     low_one_ref[...] = dot(up_one_ref[...], carried, 1, 1).astype(BF16)
     direct_ref[...] = dot(carried, weight_ref[...], 1, 1)
@@ -90,6 +94,51 @@
         blocks_ref[:, i] = jnp.concatenate([block, half], axis=1).astype(BF16)
 
 
+def pick_kernel(returned_ref, target_ref, grads_ref):
+    slots = returned_ref.shape[0]
+    is_place = lax.broadcasted_iota(jnp.int32, (slots, slots), 0) == target_ref[...]
+    place = jnp.where(is_place, 1.0, 0.0).T.astype(BF16)
+    grads_ref[...] = dot(place, returned_ref[...], 1, 0)
+
+
+def soft_kernel(own_ref, other_ref, weight_ref, soft_hbm, soft_ref, written):
+    pieces, slots, columns = soft_ref.shape
+    parts = own_ref.shape[1]
+    part = own_ref.shape[3]
+    own = own_ref[...].astype(F32)
+    other = other_ref[...].astype(F32)
+    is_even = lax.axis_index("mp") % 2 == 0
+    halves = jnp.concatenate([jnp.where(is_even, own, other), jnp.where(is_even, other, own)], axis=2)
+    arrived = jnp.concatenate([halves[:, i].reshape(slots, part) for i in range(parts)], axis=1).astype(BF16)
+    copies = []
+    for j in range(pieces):
+        soft_ref[j] = dot(arrived, weight_ref[:, j * columns : (j + 1) * columns], 1, 0).astype(BF16)
+        copies.append(
+            pltpu.make_async_copy(soft_ref.at[j], soft_hbm.at[:, pl.ds(j * columns, columns)], written.at[j])
+        )
+        copies[j].start()
+    for copy in copies:
+        copy.wait()
+
+
+def call_soft(own, other, weight):
+    readers, _, pair, _ = own.shape
+    slots, features = readers * pair * 2, weight.shape[1]
+    pieces = 4
+    return pl.pallas_call(
+        soft_kernel,
+        out_shape=jax.ShapeDtypeStruct((slots, features), BF16),
+        in_specs=[pl.BlockSpec(memory_space=pltpu.VMEM)] * 3,
+        out_specs=pl.BlockSpec(memory_space=pl.ANY),
+        scratch_shapes=[
+            pltpu.VMEM((pieces, slots, features // pieces), BF16),
+            pltpu.SemaphoreType.DMA((pieces,)),
+        ],
+        cost_estimate=pl.CostEstimate(flops=2 * slots * weight.size, transcendentals=0, bytes_accessed=2 * (slots * features + weight.size + 2 * own.size)),
+        compiler_params=pltpu.CompilerParams(vmem_limit_bytes=24 << 20),
+    )(own, other, weight)
+
+
 def on_device(enc_rows, proj_weight, row_owner, grad_in, adapter_gain, adapter_down, adapter_up):
     readers = lax.axis_size("seq")
     feature_parts = lax.axis_size("mp")
@@ -108,14 +157,14 @@
     onward, through, low_two = call_kernel(
         relay_kernel,
         [((rank, features + width + 2 * rank), BF16), ((rank, width), BF16), ((rank, slots), BF16)],
-        gathered, first, up_one, scaled,
+        gathered, first, up_one, down, adapter_gain,
     )
     onward = send_along(onward, "section", 1)
     through_zero = send_along(through, "section", 2)
     carried, low_one, direct, target, routed = call_kernel(
         functools.partial(carry_kernel, readers),
         [((slots, features), BF16), ((rank, slots), BF16), ((slots, width), F32), ((1, slots), jnp.int32), ((slots, part), BF16)],
-        row_owner, enc_block, grad, low_two, scaled, up_one, proj_weight,
+        row_owner, enc_block, grad, low_two, down, adapter_gain, up_one, proj_weight,
     )
     gathered = lax.all_gather(low_one, "mp")
     (blocks,) = call_kernel(
@@ -130,14 +179,9 @@
     returned = send_along(returned, "section", -2)
     own_half = blocks[:, :, per_peer:]
     other_half = lax.ppermute(own_half, "mp", [(i, i ^ 1) for i in range(feature_parts)])
-    is_even = lax.axis_index("mp") % 2 == 0
-    arrived = jnp.stack(
-        [jnp.where(is_even, own_half, other_half), jnp.where(is_even, other_half, own_half)], axis=1
-    )
-    arrived = arrived.transpose(0, 1, 3, 2, 4).reshape(slots, width)
-    soft_block = dot(arrived, proj_weight, 1, 0).astype(BF16)
     place = (lax.broadcasted_iota(jnp.int32, (slots, slots), 0) == target).astype(BF16)
     row_grads = dot(place, returned, 0, 0)
+    soft_block = call_soft(own_half, other_half, proj_weight)
     return soft_block[None], row_grads[None]
 
 

time: 81.2 us -> 79.3 us (0.977)
  waiting for transfers between devices: 7.76 us -> 5.26 us
  matrix products: 5.4 us -> 3.86 us
  Pallas kernels: 2.6 us -> 4.05 us
  other arithmetic: 1.09 us -> 0.05 us
  blocking collectives: 48.2 us -> 49.2 us
    ppermute x4, waiting for transfers between devices: 7.75 us -> 5.23 us  [send_along(): lax.ppermute(value, axis, [(i, (i + steps) % count) for i in range(count)])]
    dot_general x4 -> x3, matrix products: 5.4 us -> 3.86 us  [dot(): lax.dot_general(a, b, (((contract_a,), (contract_b,)), ((), ())), preferr...]
    pallas_call x0 -> x1, Pallas kernels: none -> 1.45 us  [call_soft(): pl.pallas_call(soft_kernel, out_shape=jax.ShapeDtypeStruct((slots, featur...]
    convert_element_type x1 -> x0, other arithmetic: 1 us -> none  [on_device(): scaled = (down.astype(F32) * adapter_gain).astype(BF16)]
    all_gather x1, blocking collectives: 5.42 us -> 6.25 us  [on_device(): gathered = lax.all_gather(low_one, 'mp')]
  transfers between devices with their start and end apart: 5 -> 5, of which waited for: 2 -> 1; matrix products, arithmetic and copies ran while one was open for 6% -> 5% of each run, Pallas kernels for 2% -> 2%
where the time goes in v3:
time: 79.3 us; the launch traced here: 78.2 us
  blocking collectives  49.2 us (62%)
  starting transfers between devices  14.9 us (19%)
  waiting for transfers between devices  5.26 us (7%)
  Pallas kernels  4.05 us (5%)
  matrix products  3.86 us (5%)
  between operations  0.82 us (1%)
    all_to_all x1, blocking collectives, on_device(): lax.all_to_all(blocks, ('seq', 'mp'), split_axis=0, concat_axis=0, tiled=...  25.5 us
    all_gather x1, blocking collectives, on_device(): gathered = lax.all_gather(first, 'mp')  17.4 us
    ppermute x4, starting transfers between devices, send_along(): lax.ppermute(value, axis, [(i, (i + steps) % count) for i in range(count)])  12.5 us
    all_gather x1, blocking collectives, on_device(): gathered = lax.all_gather(low_one, 'mp')  6.25 us
    ppermute x4, waiting for transfers between devices, send_along(): lax.ppermute(value, axis, [(i, (i + steps) % count) for i in range(count)])  5.23 us
    dot_general x3, matrix products, dot(): lax.dot_general(a, b, (((contract_a,), (contract_b,)), ((), ())), preferr...  3.86 us
    pallas_call x3, Pallas kernels, call_kernel(): pl.pallas_call(body, out_shape=[jax.ShapeDtypeStruct(shape, kind) for sha...  2.6 us
    ppermute x1, starting transfers between devices, on_device(): lax.ppermute(own_half, 'mp', [(i, i ^ 1) for i in range(feature_parts)])  2.46 us
  transfers between devices with their start and end apart: 5, of which 1 were waited for; matrix products, arithmetic and copies ran while one was open for 5% of the time, Pallas kernels for 2%

profile of v3, /device:TPU:1, one launch (start us, length us, event | category | flops | bytes accessed | tf_op | source)
XLA Modules:
  0.0 78.2 jit_solution(1934061221179906271)
XLA Ops:
  0.6 0.0 copy-start.6
  0.6 0.0 copy-start.1
  0.7 5.0 %collective-permute-start = (bf16[64,2048]{1,0:T(8,128)(2,1)}, bf16[64,2048]{1,0:T(8,128)(2,1)S(1)}, u32[]{:S(2)}, u32[]{:S(2)}) collective-permute-start(bf16[64,2048]{1,0:T(8,128)(2,1)} %bitcast.36), channel_id=1, source_target_pairs={{0,4},{4,8},{8,12},{12,16},{16,20},{20,24},{24,28},{28,32},{32,36}... | collective-permute-start | bytes 786440 | tf_op jit(solution)/shard_map/ppermute | solution.py:16
  5.6 0.0 copy-start.2
  5.6 0.0 copy-start.4
  5.6 2.5 %convolution_convert_fusion = bf16[64,512]{1,0:T(8,128)(2,1)S(1)} fusion(bf16[512,2048]{1,0:T(8,128)(2,1)} %weight_ref.3, f32[2048]{0:T(1024)} %bitcast.31, bf16[1,64,2048]{2,1,0:T(8,128)(2,1)} %param.12), kind=kOutput, calls=%fused_computation.1 | convolution fusion | flops 134643712 | bytes 2433024 | tf_op jit(solution)/shard_map/dot_general | solution.py:20
  8.1 0.0 copy-done.6
  8.1 0.0 copy-done.1
  8.2 0.0 copy-start
  8.2 0.0 copy-start.3
  8.2 0.0 copy-start.5
  8.2 0.4 convolution_convert_fusion.1
  8.7 17.4 %all-gather = bf16[256,768]{1,0:T(8,128)(2,1)S(1)} all-gather(bf16[64,768]{1,0:T(8,128)(2,1)S(1)} %pad_maximum_fusion.first_ref), channel_id=2, replica_groups=mesh['seq'=16,'section'=16,'mp'=4] {'mp'}, dimensions={0}, use_global_device_ids=true | all-gather | bytes 491520 | tf_op jit(solution)/shard_map/all_gather | solution.py:156
  26.0 0.0 collective-permute-done.up_one_ref
  26.0 0.0 copy-done.2
  26.0 0.0 copy-done.4
  26.0 0.2 shard_map.86
  26.3 1.9 %collective-permute-start.1 = (bf16[64,2688]{1,0:T(8,128)(2,1)S(1)}, bf16[64,2688]{1,0:T(8,128)(2,1)S(1)}, u32[]{:S(2)}, u32[]{:S(2)}) collective-permute-start(bf16[64,2688]{1,0:T(8,128)(2,1)S(1)} %get-tuple-element.12), channel_id=1, source_target_pairs={{0,4},{4,8},{8,12},{12,16},{16,20},{20,24},{24,28},{28,32},{32,36}... | collective-permute-start | bytes 1032200 | tf_op jit(solution)/shard_map/ppermute | solution.py:16
  28.2 1.9 %collective-permute-start.2 = (bf16[64,512]{1,0:T(8,128)(2,1)S(1)}, bf16[64,512]{1,0:T(8,128)(2,1)S(1)}, u32[]{:S(2)}, u32[]{:S(2)}) collective-permute-start(bf16[64,512]{1,0:T(8,128)(2,1)S(1)} %get-tuple-element.13), channel_id=1, source_target_pairs={{0,8},{4,12},{8,16},{12,20},{16,24},{20,28},{24,32},{28,36},{32,40... | collective-permute-start | bytes 196616 | tf_op jit(solution)/shard_map/ppermute | solution.py:16
  30.1 0.0 copy-done
  30.1 0.0 copy-done.3
  30.1 0.0 copy-done.5
  30.2 1.5 %shard_map.87 = (bf16[256,2048]{1,0:T(8,128)(2,1)S(1)}, bf16[64,256]{1,0:T(8,128)(2,1)S(1)}, f32[256,512]{1,0:T(8,128)S(1)}, s32[1,256]{1,0:T(1,128)S(1)}, bf16[256,128]{1,0:T(8,128)(2,1)S(1)}) custom-call(s32[1,256]{1,0:T(1,128)S(1)} %copy-done.5, bf16[256,512]{1,0:T(8,128)(2,1)S(1)} %bitcast.30, bf16[256,2048]{1,0:T(8,128)(2,1)S(1)} %bitcast.24, ...), custom_call_target="tpu_custom_call" | custom-call | tf_op jit(solution)/shard_map/pallas_call | solution.py:24
  31.7 6.3 %all-gather.1 = bf16[256,256]{1,0:T(8,128)(2,1)S(1)} all-gather(bf16[64,256]{1,0:T(8,128)(2,1)S(1)} %get-tuple-element.11), channel_id=3, replica_groups=mesh['seq'=16,'section'=16,'mp'=4] {'mp'}, dimensions={0}, use_global_device_ids=true | all-gather | bytes 163840 | tf_op jit(solution)/shard_map/all_gather | solution.py:169
  37.9 5.2 %collective-permute-done.2.through_zero_ref = bf16[64,512]{1,0:T(8,128)(2,1)S(1)} collective-permute-done((bf16[64,512]{1,0:T(8,128)(2,1)S(1)}, bf16[64,512]{1,0:T(8,128)(2,1)S(1)}, u32[]{:S(2)}, u32[]{:S(2)}) %collective-permute-start.2) | collective-permute-done | bytes 65568 | tf_op jit(solution)/shard_map/ppermute | solution.py:16
  43.1 0.0 collective-permute-done.1.onward_ref
  43.1 0.9 %shard_map.88 = bf16[16,4,24,128]{3,2,1,0:T(8,128)(2,1)S(1)} custom-call(bf16[4,64,256]{2,1,0:T(8,128)(2,1)S(1)} %bitcast.29, bf16[64,2688]{1,0:T(8,128)(2,1)S(1)} %collective-permute-done.1.onward_ref, bf16[64,512]{1,0:T(8,128)(2,1)S(1)} %collective-permute-done.2.through_zero_ref, bf16[256,2048]{1,0:T(8,128)(2,1)S(1)} %get-tuple-element.14.carried_ref, ...), custom_call_target="tpu_custom_call" | custom-call | tf_op jit(solution)/shard_map/pallas_call | solution.py:24
  44.0 25.5 %all_to_all.5 = bf16[64,24,128]{2,1,0:T(8,128)(2,1)S(1)} all-to-all(bf16[64,24,128]{2,1,0:T(8,128)(2,1)S(1)} %bitcast.27), channel_id=1, replica_groups=mesh['seq'=16,'section'=16,'mp'=4] {'seq','mp'}, dimensions={0} | all-to-all | bytes 786432 | tf_op jit(solution)/shard_map/all_to_all | solution.py:176
  69.6 3.7 %collective-permute-start.4 = (bf16[256,128]{1,0:T(8,128)(2,1)S(1)}, bf16[256,128]{1,0:T(8,128)(2,1)S(1)}, u32[]{:S(2)}, u32[]{:S(2)}) collective-permute-start(bf16[256,128]{1,0:T(8,128)(2,1)S(1)} %bitcast.37), channel_id=1, source_target_pairs={{0,56},{4,60},{8,0},{12,4},{16,8},{20,12},{24,16},{28,20},{32,24},... | collective-permute-start | bytes 196616 | tf_op jit(solution)/shard_map/ppermute | solution.py:16
  73.3 2.5 %collective-permute-start.3 = (bf16[16,4,8,128]{3,2,1,0:T(8,128)(2,1)S(1)}, bf16[16,4,8,128]{3,2,1,0:T(8,128)(2,1)S(1)}, u32[]{:S(2)}, u32[]{:S(2)}) collective-permute-start(bf16[16,4,8,128]{3,2,1,0:T(8,128)(2,1)S(1)} %slice.8.own_ref), channel_id=1, source_target_pairs={{0,1},{1,0},{2,3},{3,2},{4,5},{5,4},{6,7},{7,6},{8,9},{9,8},{10,11... | collective-permute-start | bytes 393224 | tf_op jit(solution)/shard_map/ppermute | solution.py:181
  75.8 0.0 collective-permute-done.4
  75.8 0.9 %convolution_bitcast_fusion = f32[1,256,128]{2,1,0:T(8,128)} fusion(bf16[256,128]{1,0:T(8,128)(2,1)S(1)} %collective-permute-done.4, s32[256]{0:T(256)S(1)} %bitcast.32), kind=kOutput, calls=%fused_computation | convolution fusion | flops 16842752 | bytes 197632 | tf_op jit(solution)/shard_map/dot_general | solution.py:20
  76.7 0.0 collective-permute-done.3.other_ref
  76.7 1.5 %shard_map.89 = bf16[256,2048]{1,0:T(8,128)(2,1)} custom-call(bf16[16,4,8,128]{3,2,1,0:T(8,128)(2,1)S(1)} %slice.8.own_ref, bf16[16,4,8,128]{3,2,1,0:T(8,128)(2,1)S(1)} %collective-permute-done.3.other_ref, bf16[512,2048]{1,0:T(8,128)(2,1)S(1)} %copy-done), custom_call_target="tpu_custom_call" | custom-call | flops 536870912 | bytes 3407872 | tf_op jit(solution)/shard_map/pallas_call | solution.py:128
  (3 shorter events, 0.1 us)
Async XLA Ops:
  0.6 7.5 %copy-start.6 = (bf16[1,64,2048]{2,1,0:T(8,128)(2,1)S(1)}, bf16[1,64,2048]{2,1,0:T(8,128)(2,1)}, u32[]{:S(2)}) copy-start(bf16[1,64,2048]{2,1,0:T(8,128)(2,1)} %param.13) | copy-start | bytes 786436
  0.6 7.5 %copy-start.1 = (bf16[1,256,2048]{2,1,0:T(8,128)(2,1)S(1)}, bf16[1,256,2048]{2,1,0:T(8,128)(2,1)}, u32[]{:S(2)}) copy-start(bf16[1,256,2048]{2,1,0:T(8,128)(2,1)} %param.10) | copy-start | bytes 3145732
  0.7 25.4 %collective-permute-start = (bf16[64,2048]{1,0:T(8,128)(2,1)}, bf16[64,2048]{1,0:T(8,128)(2,1)S(1)}, u32[]{:S(2)}, u32[]{:S(2)}) collective-permute-start(bf16[64,2048]{1,0:T(8,128)(2,1)} %bitcast.36), channel_id=1, source_target_pairs={{0,4},{4,8},{8,12},{12,16},{16,20},{20,24},{24,28},{28,32},{32,36}... | collective-permute-start | bytes 786440 | tf_op jit(solution)/shard_map/ppermute | solution.py:16
  5.6 20.4 %copy-start.2 = (bf16[1,64,2048]{2,1,0:T(8,128)(2,1)S(1)}, bf16[1,64,2048]{2,1,0:T(8,128)(2,1)}, u32[]{:S(2)}) copy-start(bf16[1,64,2048]{2,1,0:T(8,128)(2,1)} %param.12) | copy-start | bytes 786436
  5.6 20.4 %copy-start.4 = (f32[1,2048]{1,0:T(1,128)S(1)}, f32[1,2048]{1,0:T(1,128)}, u32[]{:S(2)}) copy-start(f32[1,2048]{1,0:T(1,128)} %gain_ref.3) | copy-start | bytes 24580
  8.2 22.0 %copy-start = (bf16[512,2048]{1,0:T(8,128)(2,1)S(1)}, bf16[512,2048]{1,0:T(8,128)(2,1)}, u32[]{:S(2)}) copy-start(bf16[512,2048]{1,0:T(8,128)(2,1)} %weight_ref.3) | copy-start | bytes 6291460
  8.2 22.0 %copy-start.3 = (bf16[1,256,512]{2,1,0:T(8,128)(2,1)S(1)}, bf16[1,256,512]{2,1,0:T(8,128)(2,1)}, u32[]{:S(2)}) copy-start(bf16[1,256,512]{2,1,0:T(8,128)(2,1)} %param.7) | copy-start | bytes 786436
  8.2 22.0 %copy-start.5 = (s32[1,256]{1,0:T(1,128)S(1)}, s32[1,256]{1,0:T(1,128)}, u32[]{:S(2)}) copy-start(s32[1,256]{1,0:T(1,128)} %owner_ref.1) | copy-start | bytes 3076
  26.3 16.9 %collective-permute-start.1 = (bf16[64,2688]{1,0:T(8,128)(2,1)S(1)}, bf16[64,2688]{1,0:T(8,128)(2,1)S(1)}, u32[]{:S(2)}, u32[]{:S(2)}) collective-permute-start(bf16[64,2688]{1,0:T(8,128)(2,1)S(1)} %get-tuple-element.12), channel_id=1, source_target_pairs={{0,4},{4,8},{8,12},{12,16},{16,20},{20,24},{24,28},{28,32},{32,36}... | collective-permute-start | bytes 1032200 | tf_op jit(solution)/shard_map/ppermute | solution.py:16
  28.2 14.9 %collective-permute-start.2 = (bf16[64,512]{1,0:T(8,128)(2,1)S(1)}, bf16[64,512]{1,0:T(8,128)(2,1)S(1)}, u32[]{:S(2)}, u32[]{:S(2)}) collective-permute-start(bf16[64,512]{1,0:T(8,128)(2,1)S(1)} %get-tuple-element.13), channel_id=1, source_target_pairs={{0,8},{4,12},{8,16},{12,20},{16,24},{20,28},{24,32},{28,36},{32,40... | collective-permute-start | bytes 196616 | tf_op jit(solution)/shard_map/ppermute | solution.py:16
  69.6 6.2 %collective-permute-start.4 = (bf16[256,128]{1,0:T(8,128)(2,1)S(1)}, bf16[256,128]{1,0:T(8,128)(2,1)S(1)}, u32[]{:S(2)}, u32[]{:S(2)}) collective-permute-start(bf16[256,128]{1,0:T(8,128)(2,1)S(1)} %bitcast.37), channel_id=1, source_target_pairs={{0,56},{4,60},{8,0},{12,4},{16,8},{20,12},{24,16},{28,20},{32,24},... | collective-permute-start | bytes 196616 | tf_op jit(solution)/shard_map/ppermute | solution.py:16
  73.3 3.4 %collective-permute-start.3 = (bf16[16,4,8,128]{3,2,1,0:T(8,128)(2,1)S(1)}, bf16[16,4,8,128]{3,2,1,0:T(8,128)(2,1)S(1)}, u32[]{:S(2)}, u32[]{:S(2)}) collective-permute-start(bf16[16,4,8,128]{3,2,1,0:T(8,128)(2,1)S(1)} %slice.8.own_ref), channel_id=1, source_target_pairs={{0,1},{1,0},{2,3},{3,2},{4,5},{5,4},{6,7},{7,6},{8,9},{9,8},{10,11... | collective-permute-start | bytes 393224 | tf_op jit(solution)/shard_map/ppermute | solution.py:181
